TPU v7x, 256 devices: a whole 4x4x8 slice. The times are simulated.
256 devices in a mesh: dp: 32 (over z, y), chan: 8 (over x, core).
Axes of the slice: x: 4, y: 4, z: 8, core: 2. Of those that a mesh axis runs over, the one named last changes fastest.
Arguments:
- inputs: bfloat16 [12544, 2048], P('dp', 'chan'), may hold values from -6 to 6
- conv_one: bfloat16 [9, 32, 2048], P(None, None, 'chan'), may hold values from -0.375 to 0.375
- conv_two: bfloat16 [9, 32, 2048], P(None, None, 'chan'), may hold values from -0.375 to 0.375
- probe_one: bfloat16 [2048, 512], P('chan'), may hold values from -0.125 to 0.125
- probe_two: bfloat16 [2048, 512], P('chan'), may hold values from -0.125 to 0.125
Outputs:
- restored: bfloat16 [12544, 2048], P('dp', 'chan')
- triangle: float32 [512, 512], replicated
All inputs are finite; a program needn't handle non-finite values.
Results may differ from a plain program's by a relative error of at most 0.028.
Values may be sent and summed in bfloat16 or wider, within the bound.
No kernel may reach another device: no remote copies, remote signals or barrier semaphores. Data moves between devices by JAX's collectives and lax.ppermute only.
A program may use at most 64 MiB of HBM per device.

v0:
```python
import math
import jax
import jax.numpy as jnp
from jax import lax
from jax.sharding import PartitionSpec as P

SIDE = 7


def convolve(field, weight):
    pixels, width = field.shape
    group_width = weight.shape[1]
    groups = width // group_width
    images = field.reshape(pixels // (SIDE * SIDE), SIDE, SIDE, width)
    padded = jnp.pad(images, ((0, 0), (1, 1), (1, 1), (0, 0)))
    total = jnp.zeros((pixels, groups, group_width), jnp.float32)
    for offset in range(9):
        row_shift = offset // 3
        col_shift = offset % 3
        window = padded[:, row_shift : row_shift + SIDE, col_shift : col_shift + SIDE, :]
        window = window.reshape(pixels, groups, group_width)
        kernel = weight[offset].reshape(group_width, groups, group_width)
        total = total + jnp.einsum(
            "pgi,igo->pgo", window, kernel, preferred_element_type=jnp.float32
        )
    return total.reshape(pixels, width).astype(jnp.bfloat16)


def gram_of(sketch):
    return lax.dot_general(
        sketch, sketch, (((0,), (0,)), ((), ())), preferred_element_type=jnp.float32
    )


def cross_of(sketch, responses):
    return lax.dot_general(
        sketch, responses, (((0,), (0,)), ((), ())), preferred_element_type=jnp.float32
    )


def finish(sketch, gram, cross):
    lower = jnp.linalg.cholesky(gram)
    coeffs = lax.linalg.triangular_solve(lower, cross, left_side=True, lower=True).astype(
        jnp.bfloat16
    )
    mapped = lax.linalg.triangular_solve(
        lower, coeffs.astype(jnp.float32), left_side=True, lower=True, transpose_a=True
    ).astype(jnp.bfloat16)
    return (jnp.dot(sketch, mapped, preferred_element_type=jnp.float32).astype(jnp.bfloat16), lower)


def compress(responses, probe):
    partial_sketch = jnp.dot(responses, probe, preferred_element_type=jnp.float32)
    sketch = lax.psum(partial_sketch, "chan").astype(jnp.bfloat16)
    gram, cross = lax.psum((gram_of(sketch), cross_of(sketch, responses)), "dp")
    return finish(sketch, gram, cross)


def per_device(inputs, conv_one, conv_two, probe_one, probe_two):
    responses_one = convolve(inputs, conv_one)
    restored_one, lower_one = compress(responses_one, probe_one)
    activated = jnp.maximum(restored_one, jnp.zeros((), jnp.bfloat16))
    responses_two = convolve(activated, conv_two)
    restored, lower_two = compress(responses_two, probe_two)
    total_rows = inputs.shape[0] * lax.axis_size("dp")
    triangle = jnp.transpose(lower_two) * (1.0 / math.sqrt(total_rows))
    return (restored, triangle)


def solution(mesh):
    in_specs = (
        P("dp", "chan"),
        P(None, None, "chan"),
        P(None, None, "chan"),
        P("chan", None),
        P("chan", None),
    )
    out_specs = (P("dp", "chan"), P())
    return jax.shard_map(
        per_device, mesh=mesh, in_specs=in_specs, out_specs=out_specs, check_vma=False
    )
```

profile of v0, /device:TPU:2, one launch (start us, length us, event | category | flops | bytes accessed | tf_op | source)
XLA Modules:
  0.0 705.7 jit_solution(17671794830554544109)
XLA Ops:
  31.8 28.5 %all-reduce.13 = bf16[392,512]{1,0:T(8,128)(2,1)S(1)} all-reduce(f32[392,512]{1,0:T(8,128)S(1)} %fusion.143), channel_id=1, replica_groups=mesh['dp'=32,'chan'=8] {'chan'}, use_global_device_ids=true, to_apply=%region_0.1 | all-reduce | flops 200704 | bytes 1204224 | tf_op jit(solution)/shard_map/psum | solution.py:54
  69.7 149.1 %all-reduce.12.cloned.1.call-done = (f32[512,256]{1,0:T(8,128)}, f32[512,512]{0,1:T(8,128)}) async-done(((f32[512,256]{1,0:T(8,128)}, f32[512,512]{0,1:T(8,128)}), (f32[512,256]{1,0:T(8,128)}, f32[512,512]{0,1:T(8,128)})) %all-reduce.12.cloned.1.call-update) | async-done | bytes 1572880 | tf_op jit(solution)/shard_map/psum | solution.py:55
  218.8 1.6 copy.60
  221.6 11.7 %cholesky.286 = f32[128,128]{1,0:T(8,128)S(1)} custom-call(f32[128,128]{1,0:T(8,128)S(1)} %cholesky.426), custom_call_target="Cholesky" | custom-call | tf_op jit(solution)/shard_map/jit(cholesky)/cholesky | solution.py:42
  233.5 9.8 %custom-call.31 = f32[1,128,128]{1,2,0:T(8,128)S(1)} custom-call(f32[1,128,128]{2,1,0:T(8,128)S(1)} %get-tuple-element.120), custom_call_target="InvertDiagBlocksLowerTriangular" | custom-call | tf_op jit(solution)/shard_map/jit(cholesky)/cholesky | solution.py:42
  244.0 11.7 %cholesky.305 = f32[128,128]{1,0:T(8,128)S(1)} custom-call(f32[128,128]{1,0:T(8,128)S(1)} %cholesky.430), custom_call_target="Cholesky" | custom-call | tf_op jit(solution)/shard_map/jit(cholesky)/cholesky | solution.py:42
  255.8 10.2 %custom-call.32 = f32[1,128,128]{1,2,0:T(8,128)S(1)} custom-call(f32[1,128,128]{2,1,0:T(8,128)S(1)} %get-tuple-element.117), custom_call_target="InvertDiagBlocksLowerTriangular" | custom-call | tf_op jit(solution)/shard_map/jit(cholesky)/cholesky | solution.py:42
  266.6 11.7 %cholesky.326 = f32[128,128]{1,0:T(8,128)S(1)} custom-call(f32[128,128]{1,0:T(8,128)S(1)} %cholesky.435), custom_call_target="Cholesky" | custom-call | tf_op jit(solution)/shard_map/jit(cholesky)/cholesky | solution.py:42
  279.1 9.8 %custom-call.33 = f32[1,128,128]{1,2,0:T(8,128)S(1)} custom-call(f32[1,128,128]{2,1,0:T(8,128)S(1)} %get-tuple-element.114), custom_call_target="InvertDiagBlocksLowerTriangular" | custom-call | tf_op jit(solution)/shard_map/jit(cholesky)/cholesky | solution.py:42
  289.5 11.9 %cholesky.343 = f32[128,128]{1,0:T(8,128)S(1)} custom-call(f32[128,128]{1,0:T(8,128)S(1)} %convolution_subtract_fusion.17), custom_call_target="Cholesky" | custom-call | tf_op jit(solution)/shard_map/jit(cholesky)/cholesky | solution.py:42
  305.5 8.4 %while.8 = (s32[]{:T(128)}, f32[512,512]{1,0:T(8,128)S(1)}, s32[4,2]{0,1:T(2,128)S(1)}, f32[4,128,128]{2,1,0:T(8,128)S(1)}, s32[]{:T(128)}) while((s32[]{:T(128)}, f32[512,512]{1,0:T(8,128)S(1)}, s32[4,2]{0,1:T(2,128)S(1)}, f32[4,128,128]{2,1,0:T(8,128)S(1)}, s32[]{:T(128)}) %tuple.96), condition=%wide.while_cond.1, body=%wide.while_body.1.sunk | while | flops 2 | bytes 131181 | solution.py:46
  313.8 39.3 %custom-call.35 = f32[4,128,128]{1,2,0:T(8,128)S(1)} custom-call(f32[4,128,128]{2,1,0:T(8,128)S(1)} %get-tuple-element.34), custom_call_target="InvertDiagBlocksLowerTriangular" | custom-call | tf_op jit(solution)/shard_map/triangular_solve/custom-call.8 | solution.py:46
  376.4 26.7 %all-reduce.14 = bf16[392,512]{1,0:T(8,128)(2,1)S(1)} all-reduce(f32[392,512]{1,0:T(8,128)S(1)} %fusion.145), channel_id=1, replica_groups=mesh['dp'=32,'chan'=8] {'chan'}, use_global_device_ids=true, to_apply=%region_11.15 | all-reduce | flops 200704 | bytes 1204224 | tf_op jit(solution)/shard_map/psum | solution.py:54
  405.7 150.2 %all-reduce.10.cloned.1.call-done = (f32[512,256]{1,0:T(8,128)}, f32[512,512]{0,1:T(8,128)}) async-done(((f32[512,256]{1,0:T(8,128)}, f32[512,512]{0,1:T(8,128)}), (f32[512,256]{1,0:T(8,128)}, f32[512,512]{0,1:T(8,128)})) %all-reduce.10.cloned.1.call-update) | async-done | bytes 1572880 | tf_op jit(solution)/shard_map/psum | solution.py:55
  555.9 1.6 copy.80
  558.8 11.7 %cholesky.358 = f32[128,128]{1,0:T(8,128)S(1)} custom-call(f32[128,128]{1,0:T(8,128)S(1)} %cholesky.439), custom_call_target="Cholesky" | custom-call | tf_op jit(solution)/shard_map/jit(cholesky)/cholesky | solution.py:42
  570.6 9.8 %custom-call.36 = f32[1,128,128]{1,2,0:T(8,128)S(1)} custom-call(f32[1,128,128]{2,1,0:T(8,128)S(1)} %get-tuple-element.110), custom_call_target="InvertDiagBlocksLowerTriangular" | custom-call | tf_op jit(solution)/shard_map/jit(cholesky)/cholesky | solution.py:42
  581.1 11.7 %cholesky.377 = f32[128,128]{1,0:T(8,128)S(1)} custom-call(f32[128,128]{1,0:T(8,128)S(1)} %cholesky.443), custom_call_target="Cholesky" | custom-call | tf_op jit(solution)/shard_map/jit(cholesky)/cholesky | solution.py:42
  594.2 9.9 %custom-call.37 = f32[1,128,128]{1,2,0:T(8,128)S(1)} custom-call(f32[1,128,128]{2,1,0:T(8,128)S(1)} %get-tuple-element.107), custom_call_target="InvertDiagBlocksLowerTriangular" | custom-call | tf_op jit(solution)/shard_map/jit(cholesky)/cholesky | solution.py:42
  604.8 11.7 %cholesky.398 = f32[128,128]{1,0:T(8,128)S(1)} custom-call(f32[128,128]{1,0:T(8,128)S(1)} %cholesky.448), custom_call_target="Cholesky" | custom-call | tf_op jit(solution)/shard_map/jit(cholesky)/cholesky | solution.py:42
  617.2 9.8 %custom-call.38 = f32[1,128,128]{1,2,0:T(8,128)S(1)} custom-call(f32[1,128,128]{2,1,0:T(8,128)S(1)} %get-tuple-element.104), custom_call_target="InvertDiagBlocksLowerTriangular" | custom-call | tf_op jit(solution)/shard_map/jit(cholesky)/cholesky | solution.py:42
  627.6 11.9 %cholesky.415 = f32[128,128]{1,0:T(8,128)S(1)} custom-call(f32[128,128]{1,0:T(8,128)S(1)} %convolution_subtract_fusion.16), custom_call_target="Cholesky" | custom-call | tf_op jit(solution)/shard_map/jit(cholesky)/cholesky | solution.py:42
  644.0 8.4 %while.9 = (s32[]{:T(128)}, f32[512,512]{1,0:T(8,128)S(1)}, s32[4,2]{0,1:T(2,128)S(1)}, f32[4,128,128]{2,1,0:T(8,128)S(1)}, s32[]{:T(128)}) while((s32[]{:T(128)}, f32[512,512]{1,0:T(8,128)S(1)}, s32[4,2]{0,1:T(2,128)S(1)}, f32[4,128,128]{2,1,0:T(8,128)S(1)}, s32[]{:T(128)}) %tuple.108), condition=%wide.while_cond.1.clone, body=%wide.while_body.1.clone.sunk | while | flops 2 | bytes 131181 | solution.py:46
  652.4 39.3 %custom-call.40 = f32[4,128,128]{1,2,0:T(8,128)S(1)} custom-call(f32[4,128,128]{2,1,0:T(8,128)S(1)} %get-tuple-element.36), custom_call_target="InvertDiagBlocksLowerTriangular" | custom-call | tf_op jit(solution)/shard_map/triangular_solve/custom-call.8 | solution.py:46
  (246 shorter events, 95.5 us)
Async XLA Ops:
  7.2 24.3 %copy-start = (bf16[256,512]{1,0:T(8,128)(2,1)S(1)}, bf16[256,512]{1,0:T(8,128)(2,1)}, u32[]{:S(2)}) copy-start(bf16[256,512]{1,0:T(8,128)(2,1)} %param.13) | copy-start | bytes 786436
  7.2 1.1 copy-start.18
  7.2 211.6 %all-reduce.12.cloned.1.call-start = ((), (), s32[]{:S(2)}) async-start(), calls=%async_computation.1 | async-start | bytes 3145728 | tf_op jit(solution)/shard_map/psum | solution.py:55
  23.5 1.3 copy-start.22
  25.3 1.2 copy-start.4
  26.1 1.2 copy-start.5
  27.5 1.3 copy-start.6
  29.4 1.1 copy-start.35
  62.8 493.0 %all-reduce.10.cloned.1.call-start = ((), (), s32[]{:S(2)}) async-start(), calls=%async_computation | async-start | bytes 3145728 | tf_op jit(solution)/shard_map/psum | solution.py:55
  218.8 1.7 copy-start.1
  221.6 21.7 %copy-start.15 = (f32[512,512]{1,0:T(8,128)S(1)}, f32[512,512]{1,0:T(8,128)}, u32[]{:S(2)}) copy-start(f32[512,512]{1,0:T(8,128)} %copy-done.14) | copy-start | bytes 3145732
  305.3 47.9 %copy-start.19 = (f32[512,256]{1,0:T(8,128)S(1)}, f32[512,256]{1,0:T(8,128)}, u32[]{:S(2)}) copy-start(f32[512,256]{1,0:T(8,128)} %get-tuple-element.59) | copy-start | bytes 1572868
  367.3 1.4 copy-start.17
  367.3 1.4 copy-start.27
  367.3 1.6 copy-start.11
  369.6 1.1 copy-start.32
  371.5 1.1 copy-start.9
  371.5 1.1 copy-start.31
  372.7 1.1 copy-start.8
  372.7 1.1 copy-start.30
  555.9 1.7 copy-start.2
  558.8 21.7 %copy-start.13 = (f32[512,512]{1,0:T(8,128)S(1)}, f32[512,512]{1,0:T(8,128)}, u32[]{:S(2)}) copy-start(f32[512,512]{1,0:T(8,128)} %copy-done.12) | copy-start | bytes 3145732
  642.8 48.9 %copy-start.20 = (f32[512,256]{1,0:T(8,128)S(1)}, f32[512,256]{1,0:T(8,128)}, u32[]{:S(2)}) copy-start(f32[512,256]{1,0:T(8,128)} %get-tuple-element.57) | copy-start | bytes 1572868
  696.1 1.2 copy-start.3
  (16 other events, 15.0 us)
Sparse Core Ops, SparseCore 0:
  63.0 155.7 all-reduce.11
  405.8 149.9 all-reduce.9
where the time goes:
time: 713 us; the launch traced here: 706 us
  waiting for transfers between devices  299 us (42%)
  other arithmetic  239 us (34%)
  local copies, waits for them, and re-layouts  62.7 us (9%)
  blocking collectives  55.2 us (8%)
  matrix products  29 us (4%)
  between operations  20.4 us (3%)
    psum x2, waiting for transfers between devices, compress(): gram, cross = lax.psum((gram_of(sketch), cross_of(sketch, responses)), 'dp')  299 us
    another operation x29, other arithmetic, finish(): lower = jnp.linalg.cholesky(gram)  158 us
    another operation x4, other arithmetic, finish(): lax.linalg.triangular_solve(lower, coeffs.astype(jnp.float32), left_side=...  78.8 us
    psum x2, blocking collectives, compress(): sketch = lax.psum(partial_sketch, 'chan').astype(jnp.bfloat16)  55.2 us
    another operation x27, local copies, waits for them, and re-layouts, finish(): lax.linalg.triangular_solve(lower, coeffs.astype(jnp.float32), left_side=...  16.6 us
    reshape x16, local copies, waits for them, and re-layouts, convolve(): window = window.reshape(pixels, groups, group_width)  14.8 us
  transfers between devices with their start and end apart: 2, of which 2 were waited for; matrix products, arithmetic and copies ran while one was open for 1% of the time, Pallas kernels for 0%

commit v1 on v0

--- a/solution.py
+++ b/solution.py
@@ -50,8 +50,12 @@
 
 
 def compress(responses, probe):
+
+    def refer_sector_over_axis(x_in, axis_name):
+        return jnp.sum(lax.all_gather(x_in, axis_name), 0)
+
     partial_sketch = jnp.dot(responses, probe, preferred_element_type=jnp.float32)
-    sketch = lax.psum(partial_sketch, "chan").astype(jnp.bfloat16)
+    sketch = refer_sector_over_axis(partial_sketch, "chan").astype(jnp.bfloat16)
     gram, cross = lax.psum((gram_of(sketch), cross_of(sketch, responses)), "dp")
     return finish(sketch, gram, cross)
 

time: 713 us -> 761 us (1.067)
  waiting for transfers between devices: 299 us -> 386 us
  blocking collectives: 55.2 us -> 0 us
  matrix products: 29 us -> 42.6 us
  other arithmetic: 239 us -> 249 us
    all_gather x0 -> x2, waiting for transfers between devices: none -> 86.2 us  [refer_sector_over_axis(): return jnp.sum(lax.all_gather(x_in, axis_name), 0)]
    psum x2 -> x0, blocking collectives: 55.2 us -> none  [compress(): sketch = lax.psum(partial_sketch, 'chan').astype(jnp.bfloat16)]
    dot_general x18, matrix products: 9.41 us -> 17.6 us  [convolve(): jnp.einsum('pgi,igo->pgo', window, kernel, preferred_element_type=jnp.flo...]
  transfers between devices with their start and end apart: 2 -> 4, of which waited for: 2 -> 4; matrix products, arithmetic and copies ran while one was open for 1% -> 1% of each run, Pallas kernels for 0% -> 0%
where the time goes in v1:
time: 761 us; the launch traced here: 754 us
  waiting for transfers between devices  386 us (51%)
  other arithmetic  249 us (33%)
  local copies, waits for them, and re-layouts  55.3 us (7%)
  matrix products  42.6 us (6%)
  between operations  20 us (3%)
    psum x2, waiting for transfers between devices, compress(): gram, cross = lax.psum((gram_of(sketch), cross_of(sketch, responses)), 'dp')  299 us
    another operation x29, other arithmetic, finish(): lower = jnp.linalg.cholesky(gram)  158 us
    all_gather x2, waiting for transfers between devices, refer_sector_over_axis(): return jnp.sum(lax.all_gather(x_in, axis_name), 0)  86.2 us
    another operation x4, other arithmetic, finish(): lax.linalg.triangular_solve(lower, coeffs.astype(jnp.float32), left_side=...  79.6 us
    dot_general x18, matrix products, convolve(): jnp.einsum('pgi,igo->pgo', window, kernel, preferred_element_type=jnp.flo...  17.6 us
    another operation x27, local copies, waits for them, and re-layouts, finish(): lax.linalg.triangular_solve(lower, coeffs.astype(jnp.float32), left_side=...  16.3 us
  transfers between devices with their start and end apart: 4, of which 4 were waited for; matrix products, arithmetic and copies ran while one was open for 1% of the time, Pallas kernels for 0%

profile of v1, /device:TPU:2, one launch (start us, length us, event | category | flops | bytes accessed | tf_op | source)
XLA Modules:
  0.0 753.9 jit_solution(16377027552630394740)
XLA Ops:
  35.4 46.2 %all-gather.5.cloned.1.call-done = f32[3136,512]{1,0:T(8,128)} async-done(((f32[392,512]{1,0:T(8,128)}), f32[3136,512]{1,0:T(8,128)}) %all-gather.5.cloned.1.call-update) | async-done | bytes 6422544 | tf_op jit(solution)/shard_map/all_gather | solution.py:55
  81.6 3.6 reduce_sum.18
  94.1 146.6 %all-reduce.10.cloned.1.call-done = (f32[512,256]{1,0:T(8,128)}, f32[512,512]{0,1:T(8,128)}) async-done(((f32[512,256]{1,0:T(8,128)}, f32[512,512]{0,1:T(8,128)}), (f32[512,256]{1,0:T(8,128)}, f32[512,512]{0,1:T(8,128)})) %all-reduce.10.cloned.1.call-update) | async-done | bytes 1572880 | tf_op jit(solution)/shard_map/psum | solution.py:59
  244.8 11.7 %cholesky.286 = f32[128,128]{1,0:T(8,128)S(1)} custom-call(f32[128,128]{1,0:T(8,128)S(1)} %cholesky.426), custom_call_target="Cholesky" | custom-call | tf_op jit(solution)/shard_map/jit(cholesky)/cholesky | solution.py:42
  256.6 9.8 %custom-call.31 = f32[1,128,128]{1,2,0:T(8,128)S(1)} custom-call(f32[1,128,128]{2,1,0:T(8,128)S(1)} %get-tuple-element.120), custom_call_target="InvertDiagBlocksLowerTriangular" | custom-call | tf_op jit(solution)/shard_map/jit(cholesky)/cholesky | solution.py:42
  269.0 11.7 %cholesky.305 = f32[128,128]{1,0:T(8,128)S(1)} custom-call(f32[128,128]{1,0:T(8,128)S(1)} %cholesky.430), custom_call_target="Cholesky" | custom-call | tf_op jit(solution)/shard_map/jit(cholesky)/cholesky | solution.py:42
  280.7 10.2 %custom-call.32 = f32[1,128,128]{1,2,0:T(8,128)S(1)} custom-call(f32[1,128,128]{2,1,0:T(8,128)S(1)} %get-tuple-element.117), custom_call_target="InvertDiagBlocksLowerTriangular" | custom-call | tf_op jit(solution)/shard_map/jit(cholesky)/cholesky | solution.py:42
  292.5 11.7 %cholesky.326 = f32[128,128]{1,0:T(8,128)S(1)} custom-call(f32[128,128]{1,0:T(8,128)S(1)} %cholesky.435), custom_call_target="Cholesky" | custom-call | tf_op jit(solution)/shard_map/jit(cholesky)/cholesky | solution.py:42
  304.9 9.8 %custom-call.33 = f32[1,128,128]{1,2,0:T(8,128)S(1)} custom-call(f32[1,128,128]{2,1,0:T(8,128)S(1)} %get-tuple-element.114), custom_call_target="InvertDiagBlocksLowerTriangular" | custom-call | tf_op jit(solution)/shard_map/jit(cholesky)/cholesky | solution.py:42
  316.2 11.9 %cholesky.343 = f32[128,128]{1,0:T(8,128)S(1)} custom-call(f32[128,128]{1,0:T(8,128)S(1)} %convolution_subtract_fusion.17), custom_call_target="Cholesky" | custom-call | tf_op jit(solution)/shard_map/jit(cholesky)/cholesky | solution.py:42
  332.1 7.9 %while.8 = (s32[]{:T(128)}, f32[512,512]{1,0:T(8,128)S(1)}, s32[4,2]{0,1:T(2,128)S(1)}, f32[4,128,128]{2,1,0:T(8,128)S(1)}, s32[]{:T(128)}) while((s32[]{:T(128)}, f32[512,512]{1,0:T(8,128)S(1)}, s32[4,2]{0,1:T(2,128)S(1)}, f32[4,128,128]{2,1,0:T(8,128)S(1)}, s32[]{:T(128)}) %tuple.96), condition=%wide.while_cond.1, body=%wide.while_body.1.sunk | while | flops 2 | bytes 131181 | solution.py:46
  340.1 39.3 %custom-call.35 = f32[4,128,128]{1,2,0:T(8,128)S(1)} custom-call(f32[4,128,128]{2,1,0:T(8,128)S(1)} %get-tuple-element.34), custom_call_target="InvertDiagBlocksLowerTriangular" | custom-call | tf_op jit(solution)/shard_map/triangular_solve/custom-call.8 | solution.py:46
  403.5 40.0 %all-gather.7.cloned.1.call-done = f32[3136,512]{1,0:T(8,128)} async-done(((f32[392,512]{1,0:T(8,128)}), f32[3136,512]{1,0:T(8,128)}) %all-gather.7.cloned.1.call-update) | async-done | bytes 6422544 | tf_op jit(solution)/shard_map/all_gather | solution.py:55
  443.5 3.6 reduce_sum.19
  449.8 152.9 %all-reduce.8.cloned.1.call-done = (f32[512,256]{1,0:T(8,128)}, f32[512,512]{0,1:T(8,128)}) async-done(((f32[512,256]{1,0:T(8,128)}, f32[512,512]{0,1:T(8,128)}), (f32[512,256]{1,0:T(8,128)}, f32[512,512]{0,1:T(8,128)})) %all-reduce.8.cloned.1.call-update) | async-done | bytes 1572880 | tf_op jit(solution)/shard_map/psum | solution.py:59
  605.7 11.7 %cholesky.358 = f32[128,128]{1,0:T(8,128)S(1)} custom-call(f32[128,128]{1,0:T(8,128)S(1)} %cholesky.439), custom_call_target="Cholesky" | custom-call | tf_op jit(solution)/shard_map/jit(cholesky)/cholesky | solution.py:42
  617.6 9.8 %custom-call.36 = f32[1,128,128]{1,2,0:T(8,128)S(1)} custom-call(f32[1,128,128]{2,1,0:T(8,128)S(1)} %get-tuple-element.110), custom_call_target="InvertDiagBlocksLowerTriangular" | custom-call | tf_op jit(solution)/shard_map/jit(cholesky)/cholesky | solution.py:42
  628.1 11.9 %cholesky.377 = f32[128,128]{1,0:T(8,128)S(1)} custom-call(f32[128,128]{1,0:T(8,128)S(1)} %cholesky.443), custom_call_target="Cholesky" | custom-call | tf_op jit(solution)/shard_map/jit(cholesky)/cholesky | solution.py:42
  641.3 9.8 %custom-call.37 = f32[1,128,128]{1,2,0:T(8,128)S(1)} custom-call(f32[1,128,128]{2,1,0:T(8,128)S(1)} %get-tuple-element.107), custom_call_target="InvertDiagBlocksLowerTriangular" | custom-call | tf_op jit(solution)/shard_map/jit(cholesky)/cholesky | solution.py:42
  651.7 11.7 %cholesky.398 = f32[128,128]{1,0:T(8,128)S(1)} custom-call(f32[128,128]{1,0:T(8,128)S(1)} %cholesky.448), custom_call_target="Cholesky" | custom-call | tf_op jit(solution)/shard_map/jit(cholesky)/cholesky | solution.py:42
  664.2 9.8 %custom-call.38 = f32[1,128,128]{1,2,0:T(8,128)S(1)} custom-call(f32[1,128,128]{2,1,0:T(8,128)S(1)} %get-tuple-element.104), custom_call_target="InvertDiagBlocksLowerTriangular" | custom-call | tf_op jit(solution)/shard_map/jit(cholesky)/cholesky | solution.py:42
  674.6 11.9 %cholesky.415 = f32[128,128]{1,0:T(8,128)S(1)} custom-call(f32[128,128]{1,0:T(8,128)S(1)} %convolution_subtract_fusion.16), custom_call_target="Cholesky" | custom-call | tf_op jit(solution)/shard_map/jit(cholesky)/cholesky | solution.py:42
  690.9 8.5 %while.9 = (s32[]{:T(128)}, f32[512,512]{1,0:T(8,128)S(1)}, s32[4,2]{0,1:T(2,128)S(1)}, f32[4,128,128]{2,1,0:T(8,128)S(1)}, s32[]{:T(128)}) while((s32[]{:T(128)}, f32[512,512]{1,0:T(8,128)S(1)}, s32[4,2]{0,1:T(2,128)S(1)}, f32[4,128,128]{2,1,0:T(8,128)S(1)}, s32[]{:T(128)}) %tuple.112), condition=%wide.while_cond.1.clone, body=%wide.while_body.1.clone.sunk | while | flops 2 | bytes 131181 | solution.py:46
  700.1 40.1 %custom-call.40 = f32[4,128,128]{1,2,0:T(8,128)S(1)} custom-call(f32[4,128,128]{2,1,0:T(8,128)} %copy-done.11), custom_call_target="InvertDiagBlocksLowerTriangular" | custom-call | tf_op jit(solution)/shard_map/triangular_solve/custom-call.8 | solution.py:46
  (216 shorter events, 107.9 us)
Async XLA Ops:
  7.2 27.0 %copy-start = (bf16[256,512]{1,0:T(8,128)(2,1)S(1)}, bf16[256,512]{1,0:T(8,128)(2,1)}, u32[]{:S(2)}) copy-start(bf16[256,512]{1,0:T(8,128)(2,1)} %param.13) | copy-start | bytes 786436
  7.2 74.4 %all-gather.5.cloned.1.call-start = ((), (), s32[]{:S(2)}) async-start(), calls=%async_computation | async-start | bytes 7225344 | tf_op jit(solution)/shard_map/all_gather | solution.py:55
  25.2 7.2 copy-start.8
  25.3 7.2 copy-start.13
  25.3 7.4 copy-start.3
  25.3 7.4 copy-start.17
  25.3 7.9 %copy-start.4 = (bf16[392,8,32]{2,1,0:T(8,128)(2,1)S(1)}, bf16[392,8,32]{2,1,0:T(8,128)(2,1)}, u32[]{:S(2)}) copy-start(bf16[392,8,32]{2,1,0:T(8,128)(2,1)} %reshape.120) | copy-start | bytes 602116
  25.3 7.9 %copy-start.18 = (bf16[1,32,256]{1,2,0:T(8,128)(2,1)S(1)}, bf16[1,32,256]{1,2,0:T(8,128)(2,1)}, u32[]{:S(2)}) copy-start(bf16[1,32,256]{1,2,0:T(8,128)(2,1)} %copy.45) | copy-start | bytes 49156
  35.4 52.8 %copy-start.19 = (bf16[9,32,256]{2,1,0:T(8,128)(2,1)S(1)}, bf16[9,32,256]{2,1,0:T(8,128)(2,1)}, u32[]{:S(2)}) copy-start(bf16[9,32,256]{2,1,0:T(8,128)(2,1)} %param.12) | copy-start | bytes 442372
  35.4 205.3 %all-reduce.10.cloned.1.call-start = ((), (), s32[]{:S(2)}) async-start(), calls=%async_computation.3 | async-start | bytes 3145728 | tf_op jit(solution)/shard_map/psum | solution.py:59
  87.9 355.6 %all-gather.7.cloned.1.call-start = ((), (), s32[]{:S(2)}) async-start(), calls=%async_computation.1 | async-start | bytes 7225344 | tf_op jit(solution)/shard_map/all_gather | solution.py:55
  240.7 138.7 %copy-start.9 = (f32[512,256]{1,0:T(8,128)S(1)}, f32[512,256]{1,0:T(8,128)}, u32[]{:S(2)}) copy-start(f32[512,256]{1,0:T(8,128)} %get-tuple-element.59) | copy-start | bytes 1572868
  243.8 1.0 copy-start.7
  392.9 7.0 copy-start.6
  392.9 7.0 copy-start.16
  392.9 7.5 copy-start.5
  392.9 7.5 copy-start.15
  392.9 8.0 %copy-start.14 = (bf16[1,32,256]{1,2,0:T(8,128)(2,1)S(1)}, bf16[1,32,256]{1,2,0:T(8,128)(2,1)}, u32[]{:S(2)}) copy-start(bf16[1,32,256]{1,2,0:T(8,128)(2,1)} %copy.75) | copy-start | bytes 49156
  395.4 6.4 copy-start.12
  403.0 199.6 %all-reduce.8.cloned.1.call-start = ((), (), s32[]{:S(2)}) async-start(), calls=%async_computation.2 | async-start | bytes 3145728 | tf_op jit(solution)/shard_map/psum | solution.py:59
  604.2 136.0 %copy-start.10 = (f32[512,256]{1,0:T(8,128)S(1)}, f32[512,256]{1,0:T(8,128)}, u32[]{:S(2)}) copy-start(f32[512,256]{1,0:T(8,128)} %get-tuple-element.57) | copy-start | bytes 1572868
  689.8 57.3 %copy-start.1 = (bf16[256,512]{1,0:T(8,128)(2,1)S(1)}, bf16[256,512]{1,0:T(8,128)(2,1)}, u32[]{:S(2)}) copy-start(bf16[256,512]{1,0:T(8,128)(2,1)} %param.13) | copy-start | bytes 786436
  690.9 54.9 %copy-start.2 = (f32[512,512]{0,1:T(8,128)S(1)}, f32[512,512]{0,1:T(8,128)}, u32[]{:S(2)}) copy-start(f32[512,512]{0,1:T(8,128)} %get-tuple-element.65) | copy-start | bytes 3145732
  699.4 0.7 copy-start.11
Sparse Core Ops, SparseCore 0:
  35.5 46.0 all-gather.4
  88.0 152.6 all-reduce.9
  403.1 40.3 all-gather.6
  449.9 152.6 all-reduce.7
